TPU v7x, 128 devices: a whole 4x4x4 slice. The times are simulated.
128 devices in a mesh: pb: 16 (over z_hi, y, core), ka: 8 (over z_lo, x).
Axes of the slice: x: 4, y: 4, z: 4 (z_hi: 2, z_lo: 2; z = z_hi * 2 + z_lo), core: 2. Of those that a mesh axis runs over, the one named last changes fastest.
Arguments:
- query_features: bfloat16 [128, 192, 256], P('pb'), may hold values from -6 to 6
- key_features: bfloat16 [192, 128, 256], P(None, 'ka'), may hold values from -6 to 6
- pyramid_grad: bfloat16 [24576, 8, 4080], P('pb', 'ka'), may hold values from -13.0639453 to 13.0639453
- query_image: bfloat16 [128, 192, 256], P('pb', 'ka'), may hold values from -0.0625 to 0.0625
- key_image: bfloat16 [192, 128, 256], P('pb', 'ka'), may hold values from -0.0625 to 0.0625
- conv_weight: bfloat16 [3, 3, 256, 256], replicated, may hold values from -0.125 to 0.125
Outputs:
- query_image_grad: bfloat16 [128, 192, 256], P('pb', 'ka')
- key_image_grad: bfloat16 [192, 128, 256], P('pb', 'ka')
- weight_grad: float32 [3, 3, 256, 256], replicated
All inputs are finite; a program needn't handle non-finite values.
Results may differ from a plain program's by a relative error of at most 0.0056.
Values may be sent and summed in bfloat16 or wider, within the bound.
A program may use at most 128 MiB of HBM per device.

v0:
```python
import jax
import jax.numpy as jnp
from jax import lax
from jax.sharding import PartitionSpec as P

D = 256
LEVELS = 4


def padded(cells, sides, width):
    for axis, dim in sides:
        count = lax.axis_size(axis)
        ends = count - 1
        head = lax.slice_in_dim(cells, 0, width, axis=dim)
        tail = lax.slice_in_dim(cells, cells.shape[dim] - width, cells.shape[dim], axis=dim)
        cells = jnp.concatenate(
            [
                lax.ppermute(tail, axis, [(i, (i + 1) % count) for i in range(ends)]),
                cells,
                lax.ppermute(head, axis, [((i + 1) % count, i) for i in range(ends)]),
            ],
            axis=dim,
        )
    return cells


def pool_levels(strip):
    strip_float = strip.astype(jnp.float32)
    result = []
    for level_index in range(LEVELS):
        factor = 2**level_index
        cell_cols, key_rows, channels = strip_float.shape
        pooled = strip_float.reshape(
            cell_cols // factor, factor, key_rows // factor, factor, channels
        ).mean(axis=(1, 3))
        result.append(pooled.astype(jnp.bfloat16))
    return result


def conv_backward(padded_input, padded_grad, kernel):
    tile_rows = padded_grad.shape[0] - 2
    tile_cols = padded_grad.shape[1] - 2
    out_channels = padded_grad.shape[2]
    in_channels = kernel.shape[2]
    interior = padded_grad[1 : 1 + tile_rows, 1 : 1 + tile_cols].reshape(-1, out_channels)
    input_acc = jnp.zeros((tile_rows * tile_cols, in_channels), jnp.float32)
    kernel_rows = []
    for row_shift in range(3):
        kernel_row = []
        for col_shift in range(3):
            shifted = padded_grad[
                2 - row_shift : 2 - row_shift + tile_rows, 2 - col_shift : 2 - col_shift + tile_cols
            ].reshape(-1, out_channels)
            input_acc = input_acc + lax.dot_general(
                shifted,
                kernel[row_shift, col_shift],
                (((1,), (1,)), ((), ())),
                preferred_element_type=jnp.float32,
            )
            window = padded_input[
                row_shift : row_shift + tile_rows, col_shift : col_shift + tile_cols
            ].reshape(-1, in_channels)
            weight_term = lax.dot_general(
                window, interior, (((0,), (0,)), ((), ())), preferred_element_type=jnp.float32
            )
            kernel_row.append(weight_term)
        kernel_rows.append(jnp.stack(kernel_row))
    return (input_acc.reshape(tile_rows, tile_cols, in_channels), jnp.stack(kernel_rows))


def body(query_features, key_features, pyramid_grad, query_image, key_image, conv_weight):
    norm_scale = D ** (-0.5)
    strip_rows, width_cells, channels = query_features.shape
    key_rows = key_features.shape[1]
    queries = query_features.reshape(strip_rows * width_cells, channels)
    strip_grads = pyramid_grad.reshape(pyramid_grad.shape[0], pyramid_grad.shape[2])
    pooled = pool_levels(key_features)
    query_part = jnp.zeros((queries.shape[0], channels), jnp.float32)
    coarse_sum = jnp.zeros((width_cells, key_rows, channels), jnp.float32)
    level_zero = None
    offset = 0
    for level_index in range(LEVELS):
        factor = 2**level_index
        grid_rows = key_rows // factor
        grid_cols = width_cells // factor
        cell_count = grid_rows * grid_cols
        grad_block = strip_grads[:, offset : offset + cell_count]
        offset = offset + cell_count
        ordered = jnp.transpose(pooled[level_index], (1, 0, 2)).reshape(cell_count, channels)
        query_part = query_part + jnp.dot(grad_block, ordered, preferred_element_type=jnp.float32)
        if level_index == 0:
            level_zero = grad_block.reshape(-1, grid_rows, grid_cols)
        else:
            coarse = lax.dot_general(
                grad_block, queries, (((0,), (0,)), ((), ())), preferred_element_type=jnp.float32
            )
            coarse = jnp.transpose(coarse.reshape(grid_rows, grid_cols, channels), (1, 0, 2))
            spread = jnp.broadcast_to(
                coarse[:, None, :, None, :], (grid_cols, factor, grid_rows, factor, channels)
            ).reshape(width_cells, key_rows, channels)
            coarse_sum = coarse_sum + spread / 4.0**level_index
    query_grad = lax.psum_scatter(
        (query_part * norm_scale).reshape(strip_rows, width_cells, channels),
        "ka",
        scatter_dimension=1,
        tiled=True,
    ).astype(jnp.bfloat16)
    fine_term = jnp.einsum("qhw,qd->whd", level_zero, queries, preferred_element_type=jnp.float32)
    key_grad = lax.psum_scatter(
        (fine_term + coarse_sum) * norm_scale, "pb", scatter_dimension=0, tiled=True
    ).astype(jnp.bfloat16)
    padded_query_image, padded_query_grad, padded_key_image, padded_key_grad = (
        padded(query_image, (("pb", 0), ("ka", 1)), 1),
        padded(query_grad, (("pb", 0), ("ka", 1)), 1),
        padded(key_image, (("pb", 0), ("ka", 1)), 1),
        padded(key_grad, (("pb", 0), ("ka", 1)), 1),
    )
    kernel_swapped = jnp.transpose(conv_weight, (1, 0, 2, 3))
    grad_first, weight_first = conv_backward(padded_query_image, padded_query_grad, conv_weight)
    grad_second, weight_swapped = conv_backward(padded_key_image, padded_key_grad, kernel_swapped)
    local_weight = weight_first + jnp.transpose(weight_swapped, (1, 0, 2, 3))
    weight_grad = lax.psum(local_weight, ("pb", "ka"))
    return (grad_first.astype(jnp.bfloat16), grad_second.astype(jnp.bfloat16), weight_grad)


def solution(mesh):
    placed = (
        P("pb", None, None),
        P(None, "ka", None),
        P("pb", "ka", None),
        P("pb", "ka", None),
        P("pb", "ka", None),
        P(),
    )
    return jax.shard_map(
        body,
        mesh=mesh,
        in_specs=placed,
        out_specs=(P("pb", "ka", None), P("pb", "ka", None), P()),
        check_vma=False,
    )
```

profile of v0, /device:TPU:1, one launch (start us, length us, event | category | flops | bytes accessed | tf_op | source)
XLA Modules:
  0.0 347.2 jit_solution(3468012486653483771)
XLA Ops:
  7.2 4.6 %reshape.140 = f32[96,2,8,2,256]{4,3,2,1,0:T(2,128)} reshape(bf16[192,16,256]{2,1,0:T(8,128)(2,1)} %param.7) | data formatting | bytes 4718592 | tf_op jit(solution)/shard_map/reshape | solution.py:33
  11.8 1.7 copy.47
  13.5 2.5 reshape.142
  16.0 2.2 convert_element_type.43
  18.2 4.4 %reduce_sum.27 = f32[96,8,256]{2,1,0:T(8,128)S(1)} reduce(f32[96,2,8,2,256]{4,3,2,1,0:T(2,128)} %reshape.140, f32[]{:T(128)} %constant.6.clone.1), dimensions={1,3}, to_apply=%region_0.0 | reduce | flops 589824 | bytes 3932164 | tf_op jit(solution)/shard_map/reduce_sum | solution.py:35
  22.7 3.0 reduce_sum.32
  25.8 2.4 reduce_sum.33
  28.2 2.8 convolution_bitcast_fusion.2
  31.1 5.2 %fusion.4 = f32[1536,256]{1,0:T(8,128)S(1)} fusion(f32[1536,256]{1,0:T(8,128)S(1)} %convolution_bitcast_fusion.2, bf16[3072,256]{1,0:T(8,128)(2,1)S(1)} %bitcast.277, bf16[1536,4080]{0,1:T(8,128)(2,1)} %bitcast.279), kind=kOutput, calls=%fused_computation.5 | convolution fusion | flops 2416312320 | bytes 14155776 | tf_op jit(solution)/shard_map/dot_general | solution.py:90
  36.3 1.5 fusion.9
  37.8 2.5 fusion.8
  41.2 4.6 %collective-permute-start.12 = (bf16[1,16,256]{2,1,0:T(8,128)(2,1)S(1)}, bf16[1,16,256]{2,1,0:T(8,128)(2,1)S(1)}, u32[]{:S(2)}, u32[]{:S(2)}) collective-permute-start(bf16[1,16,256]{2,1,0:T(8,128)(2,1)S(1)} %get-tuple-element.28), channel_id=1, source_target_pairs={{0,8},{8,16},{16,24},{24,32},{32,40},{40,48},{48,56},{56,64},{64,7... | collective-permute-start | bytes 24584 | tf_op jit(solution)/shard_map/ppermute | solution.py:18
  45.8 1.9 collective-permute-start.13
  47.7 3.6 %collective-permute-start.8 = (bf16[1,24,256]{2,1,0:T(8,128)(2,1)S(1)}, bf16[1,24,256]{2,1,0:T(8,128)(2,1)S(1)}, u32[]{:S(2)}, u32[]{:S(2)}) collective-permute-start(bf16[1,24,256]{2,1,0:T(8,128)(2,1)S(1)} %get-tuple-element.30), channel_id=1, source_target_pairs={{0,8},{8,16},{16,24},{24,32},{32,40},{40,48},{48,56},{56,64},{64,7... | collective-permute-start | bytes 36872 | tf_op jit(solution)/shard_map/ppermute | solution.py:18
  51.4 2.1 collective-permute-start.9
  53.5 1.8 slice.313
  55.3 1.1 slice.314
  58.1 2.9 broadcast_in_dim.6
  61.1 5.3 %div.61 = f32[192,16,256]{2,0,1:T(8,128)} reshape(f32[96,2,8,2,256]{4,1,0,3,2:T(2,128)} %broadcast_in_dim.6) | data formatting | bytes 6291456 | tf_op jit(solution)/shard_map/div | solution.py:101
  66.7 2.3 broadcast_in_dim.7
  69.0 5.0 %div.65 = f32[192,16,256]{2,0,1:T(8,128)} reshape(f32[48,4,4,4,256]{4,1,0,3,2:T(4,128)} %broadcast_in_dim.7) | data formatting | bytes 6291456 | tf_op jit(solution)/shard_map/div | solution.py:101
  74.2 5.4 %fusion = f32[256,3072]{0,1:S(1)} fusion(bf16[1536,256]{1,0:T(8,128)(2,1)S(1)} %bitcast.256, bf16[1536,4080]{0,1:T(8,128)(2,1)} %bitcast.285), kind=kOutput, calls=%fused_computation | convolution fusion | flops 2415919104 | bytes 13369344
  79.9 1.6 copy-done.3
  81.5 1.0 add_multiply_fusion
  82.4 3.5 copy.54
  86.1 3.7 %collective-permute-start.14 = (bf16[14,1,256]{2,1,0:T(2,128)(2,1)S(1)}, bf16[14,1,256]{2,1,0:T(2,128)(2,1)}, u32[]{:S(2)}, u32[]{:S(2)}) collective-permute-start(bf16[14,1,256]{2,1,0:T(2,128)(2,1)S(1)} %get-tuple-element.21), channel_id=1, source_target_pairs={{0,1},{1,2},{2,3},{3,4},{4,5},{5,6},{6,7},{8,9},{9,10},{10,11},{11... | collective-permute-start | bytes 21512 | tf_op jit(solution)/shard_map/ppermute | solution.py:18
  89.8 1.3 collective-permute-start.15
  91.2 1.3 collective-permute-start.11
  92.5 4.6 %collective-permute-start.10 = (bf16[10,1,256]{2,1,0:T(2,128)(2,1)S(1)}, bf16[10,1,256]{2,1,0:T(2,128)(2,1)S(1)}, u32[]{:S(2)}, u32[]{:S(2)}) collective-permute-start(bf16[10,1,256]{2,1,0:T(2,128)(2,1)S(1)} %get-tuple-element.15), channel_id=1, source_target_pairs={{0,1},{1,2},{2,3},{3,4},{4,5},{5,6},{6,7},{8,9},{9,10},{10,11},{11... | collective-permute-start | bytes 15368 | tf_op jit(solution)/shard_map/ppermute | solution.py:18
  97.1 0.9 convert_element_type.50
  98.1 4.5 %collective-permute-start = (bf16[1,24,256]{2,1,0:T(8,128)(2,1)S(1)}, bf16[1,24,256]{2,1,0:T(8,128)(2,1)S(1)}, u32[]{:S(2)}, u32[]{:S(2)}) collective-permute-start(bf16[1,24,256]{2,1,0:T(8,128)(2,1)S(1)} %get-tuple-element.37), channel_id=1, source_target_pairs={{0,8},{8,16},{16,24},{24,32},{32,40},{40,48},{48,56},{56,64},{64,7... | collective-permute-start | bytes 36872 | tf_op jit(solution)/shard_map/ppermute | solution.py:18
  102.6 1.9 collective-permute-start.1
  106.0 1.1 maximum_bitcast_fusion.1
  107.9 1.4 collective-permute-start.2
  109.3 4.3 %collective-permute-start.3 = (bf16[10,1,256]{2,1,0:T(2,128)(2,1)S(1)}, bf16[10,1,256]{2,1,0:T(2,128)(2,1)S(1)}, u32[]{:S(2)}, u32[]{:S(2)}) collective-permute-start(bf16[10,1,256]{2,1,0:T(2,128)(2,1)S(1)} %get-tuple-element.20), channel_id=1, source_target_pairs={{0,1},{1,2},{2,3},{3,4},{4,5},{5,6},{6,7},{8,9},{9,10},{10,11},{11... | collective-permute-start | bytes 15368 | tf_op jit(solution)/shard_map/ppermute | solution.py:18
  116.9 49.9 %reduce-scatter.5.cloned.1.call-done = f32[12,16,256]{2,1,0:T(8,128)} async-done(((f32[192,16,256]{2,1,0:T(8,128)}), f32[12,16,256]{2,1,0:T(8,128)}) %reduce-scatter.5.cloned.1.call-update) | async-done | bytes 196624 | tf_op jit(solution)/shard_map/reduce_scatter | solution.py:109
  166.8 0.9 convert_element_type.53
  168.0 4.9 %collective-permute-start.4 = (bf16[1,16,256]{2,1,0:T(8,128)(2,1)S(1)}, bf16[1,16,256]{2,1,0:T(8,128)(2,1)S(1)}, u32[]{:S(2)}, u32[]{:S(2)}) collective-permute-start(bf16[1,16,256]{2,1,0:T(8,128)(2,1)S(1)} %get-tuple-element.33), channel_id=1, source_target_pairs={{0,8},{8,16},{16,24},{24,32},{32,40},{40,48},{48,56},{56,64},{64,7... | collective-permute-start | bytes 24584 | tf_op jit(solution)/shard_map/ppermute | solution.py:18
  172.9 1.9 collective-permute-start.5
  175.1 0.9 convolution_bitcast_fusion.7
  178.0 0.9 convolution_bitcast_fusion.12
  179.9 0.9 convolution_bitcast_fusion.9
  181.2 1.0 copy-done.6
  182.2 1.7 maximum_add_fusion
  184.0 1.3 collective-permute-start.6
  185.3 4.0 %collective-permute-start.7 = (bf16[14,1,256]{2,1,0:T(2,128)(2,1)S(1)}, bf16[14,1,256]{2,1,0:T(2,128)(2,1)S(1)}, u32[]{:S(2)}, u32[]{:S(2)}) collective-permute-start(bf16[14,1,256]{2,1,0:T(2,128)(2,1)S(1)} %get-tuple-element.26), channel_id=1, source_target_pairs={{0,1},{1,2},{2,3},{3,4},{4,5},{5,6},{6,7},{8,9},{9,10},{10,11},{11... | collective-permute-start | bytes 21512 | tf_op jit(solution)/shard_map/ppermute | solution.py:18
  192.6 144.7 %all-reduce.2.cloned.1.call-done = f32[3,3,256,256]{3,2,1,0:T(8,128)} async-done(((f32[3,3,256,256]{3,2,1,0:T(8,128)}), f32[3,3,256,256]{3,2,1,0:T(8,128)}) %all-reduce.2.cloned.1.call-update) | async-done | bytes 2359312 | tf_op jit(solution)/shard_map/psum | solution.py:122
  337.4 3.3 copy.73
  (114 shorter events, 16.3 us)
Async XLA Ops:
  7.2 50.2 %copy-start = (bf16[8,192,256]{2,1,0:T(8,128)(2,1)S(1)}, bf16[8,192,256]{2,1,0:T(8,128)(2,1)}, u32[]{:S(2)}) copy-start(bf16[8,192,256]{2,1,0:T(8,128)(2,1)} %param.6) | copy-start | bytes 2359300
  7.2 4.7 %copy-start.2 = (bf16[192,16,256]{2,1,0:T(8,128)(2,1)S(1)}, bf16[192,16,256]{2,1,0:T(8,128)(2,1)}, u32[]{:S(2)}) copy-start(bf16[192,16,256]{2,1,0:T(8,128)(2,1)} %param.7) | copy-start | bytes 4718596
  7.2 90.0 %reduce-scatter.3.cloned.1.call-start = ((), (), s32[]{:S(2)}) async-start(), calls=%async_computation.2 | async-start | bytes 1769472 | tf_op jit(solution)/shard_map/reduce_scatter | solution.py:102
  28.2 2.8 copy-start.7
  40.3 0.9 copy-start.9
  40.3 7.4 %copy-start.8 = (bf16[8,24,256]{2,1,0:T(8,128)(2,1)S(1)}, bf16[8,24,256]{2,1,0:T(8,128)(2,1)}, u32[]{:S(2)}) copy-start(bf16[8,24,256]{2,1,0:T(8,128)(2,1)} %param.9) | copy-start | bytes 294916
  40.3 126.4 %reduce-scatter.5.cloned.1.call-start = ((), (), s32[]{:S(2)}) async-start(), calls=%async_computation.3 | async-start | bytes 3342336 | tf_op jit(solution)/shard_map/reduce_scatter | solution.py:109
  41.2 44.8 %collective-permute-start.12 = (bf16[1,16,256]{2,1,0:T(8,128)(2,1)S(1)}, bf16[1,16,256]{2,1,0:T(8,128)(2,1)S(1)}, u32[]{:S(2)}, u32[]{:S(2)}) collective-permute-start(bf16[1,16,256]{2,1,0:T(8,128)(2,1)S(1)} %get-tuple-element.28), channel_id=1, source_target_pairs={{0,8},{8,16},{16,24},{24,32},{32,40},{40,48},{48,56},{56,64},{64,7... | collective-permute-start | bytes 24584 | tf_op jit(solution)/shard_map/ppermute | solution.py:18
  45.8 40.2 %collective-permute-start.13 = (bf16[1,16,256]{2,1,0:T(8,128)(2,1)S(1)}, bf16[1,16,256]{2,1,0:T(8,128)(2,1)S(1)}, u32[]{:S(2)}, u32[]{:S(2)}) collective-permute-start(bf16[1,16,256]{2,1,0:T(8,128)(2,1)S(1)} %get-tuple-element.27), channel_id=1, source_target_pairs={{8,0},{16,8},{24,16},{32,24},{40,32},{48,40},{56,48},{64,56},{72,6... | collective-permute-start | bytes 24584 | tf_op jit(solution)/shard_map/ppermute | solution.py:20
  47.7 43.4 %collective-permute-start.8 = (bf16[1,24,256]{2,1,0:T(8,128)(2,1)S(1)}, bf16[1,24,256]{2,1,0:T(8,128)(2,1)S(1)}, u32[]{:S(2)}, u32[]{:S(2)}) collective-permute-start(bf16[1,24,256]{2,1,0:T(8,128)(2,1)S(1)} %get-tuple-element.30), channel_id=1, source_target_pairs={{0,8},{8,16},{16,24},{24,32},{32,40},{40,48},{48,56},{56,64},{64,7... | collective-permute-start | bytes 36872 | tf_op jit(solution)/shard_map/ppermute | solution.py:18
  51.4 39.8 %collective-permute-start.9 = (bf16[1,24,256]{2,1,0:T(8,128)(2,1)S(1)}, bf16[1,24,256]{2,1,0:T(8,128)(2,1)S(1)}, u32[]{:S(2)}, u32[]{:S(2)}) collective-permute-start(bf16[1,24,256]{2,1,0:T(8,128)(2,1)S(1)} %get-tuple-element.29), channel_id=1, source_target_pairs={{8,0},{16,8},{24,16},{32,24},{40,32},{48,40},{56,48},{64,56},{72,6... | collective-permute-start | bytes 36872 | tf_op jit(solution)/shard_map/ppermute | solution.py:20
  74.2 5.7 %copy-start.4 = (f32[192,16,256]{2,0,1:T(8,128)S(1)}, f32[192,16,256]{2,0,1:T(8,128)}, u32[]{:S(2)}) copy-start(f32[192,16,256]{2,0,1:T(8,128)} %div.65) | copy-start | bytes 9437188
  79.6 1.9 copy-start.3
  85.9 251.4 %all-reduce.2.cloned.1.call-start = ((), (), s32[]{:S(2)}) async-start(), calls=%async_computation.4 | async-start | bytes 4718592 | tf_op jit(solution)/shard_map/psum | solution.py:122
  86.0 19.2 %copy-start.11 = (bf16[14,16,256]{2,1,0:T(8,128)(2,1)}, bf16[14,16,256]{2,1,0:T(8,128)(2,1)S(1)}, u32[]{:S(2)}) copy-start(bf16[14,16,256]{2,1,0:T(8,128)(2,1)S(1)} %constant_dynamic-update-slice_fusion.3) | copy-start | bytes 344068
  86.1 89.9 %collective-permute-start.14 = (bf16[14,1,256]{2,1,0:T(2,128)(2,1)S(1)}, bf16[14,1,256]{2,1,0:T(2,128)(2,1)}, u32[]{:S(2)}, u32[]{:S(2)}) collective-permute-start(bf16[14,1,256]{2,1,0:T(2,128)(2,1)S(1)} %get-tuple-element.21), channel_id=1, source_target_pairs={{0,1},{1,2},{2,3},{3,4},{4,5},{5,6},{6,7},{8,9},{9,10},{10,11},{11... | collective-permute-start | bytes 21512 | tf_op jit(solution)/shard_map/ppermute | solution.py:18
  89.8 85.2 %collective-permute-start.15 = (bf16[14,1,256]{2,1,0:T(2,128)(2,1)S(1)}, bf16[14,1,256]{2,1,0:T(2,128)(2,1)}, u32[]{:S(2)}, u32[]{:S(2)}) collective-permute-start(bf16[14,1,256]{2,1,0:T(2,128)(2,1)S(1)} %get-tuple-element.22), channel_id=1, source_target_pairs={{1,0},{2,1},{3,2},{4,3},{5,4},{6,5},{7,6},{9,8},{10,9},{11,10},{12... | collective-permute-start | bytes 21512 | tf_op jit(solution)/shard_map/ppermute | solution.py:20
  91.2 11.4 %collective-permute-start.11 = (bf16[10,1,256]{2,1,0:T(2,128)(2,1)S(1)}, bf16[10,1,256]{2,1,0:T(2,128)(2,1)S(1)}, u32[]{:S(2)}, u32[]{:S(2)}) collective-permute-start(bf16[10,1,256]{2,1,0:T(2,128)(2,1)S(1)} %get-tuple-element.16), channel_id=1, source_target_pairs={{1,0},{2,1},{3,2},{4,3},{5,4},{6,5},{7,6},{9,8},{10,9},{11,10},{12... | collective-permute-start | bytes 15368 | tf_op jit(solution)/shard_map/ppermute | solution.py:20
  92.5 12.5 %collective-permute-start.10 = (bf16[10,1,256]{2,1,0:T(2,128)(2,1)S(1)}, bf16[10,1,256]{2,1,0:T(2,128)(2,1)S(1)}, u32[]{:S(2)}, u32[]{:S(2)}) collective-permute-start(bf16[10,1,256]{2,1,0:T(2,128)(2,1)S(1)} %get-tuple-element.15), channel_id=1, source_target_pairs={{0,1},{1,2},{2,3},{3,4},{4,5},{5,6},{6,7},{8,9},{9,10},{10,11},{11... | collective-permute-start | bytes 15368 | tf_op jit(solution)/shard_map/ppermute | solution.py:18
  98.1 9.7 %collective-permute-start = (bf16[1,24,256]{2,1,0:T(8,128)(2,1)S(1)}, bf16[1,24,256]{2,1,0:T(8,128)(2,1)S(1)}, u32[]{:S(2)}, u32[]{:S(2)}) collective-permute-start(bf16[1,24,256]{2,1,0:T(8,128)(2,1)S(1)} %get-tuple-element.37), channel_id=1, source_target_pairs={{0,8},{8,16},{16,24},{24,32},{32,40},{40,48},{48,56},{56,64},{64,7... | collective-permute-start | bytes 36872 | tf_op jit(solution)/shard_map/ppermute | solution.py:18
  102.6 5.2 %collective-permute-start.1 = (bf16[1,24,256]{2,1,0:T(8,128)(2,1)S(1)}, bf16[1,24,256]{2,1,0:T(8,128)(2,1)S(1)}, u32[]{:S(2)}, u32[]{:S(2)}) collective-permute-start(bf16[1,24,256]{2,1,0:T(8,128)(2,1)S(1)} %get-tuple-element.38), channel_id=1, source_target_pairs={{8,0},{16,8},{24,16},{32,24},{40,32},{48,40},{56,48},{64,56},{72,6... | collective-permute-start | bytes 36872 | tf_op jit(solution)/shard_map/ppermute | solution.py:20
  107.5 6.1 %copy-start.5 = (bf16[3,3,256,256]{3,2,1,0:T(8,128)(2,1)S(1)}, bf16[3,3,256,256]{3,2,1,0:T(8,128)(2,1)}, u32[]{:S(2)}) copy-start(bf16[3,3,256,256]{3,2,1,0:T(8,128)(2,1)} %param.11) | copy-start | bytes 3538948
  107.9 6.0 %collective-permute-start.2 = (bf16[10,1,256]{2,1,0:T(2,128)(2,1)S(1)}, bf16[10,1,256]{2,1,0:T(2,128)(2,1)S(1)}, u32[]{:S(2)}, u32[]{:S(2)}) collective-permute-start(bf16[10,1,256]{2,1,0:T(2,128)(2,1)S(1)} %get-tuple-element.19), channel_id=1, source_target_pairs={{1,0},{2,1},{3,2},{4,3},{5,4},{6,5},{7,6},{9,8},{10,9},{11,10},{12... | collective-permute-start | bytes 15368 | tf_op jit(solution)/shard_map/ppermute | solution.py:20
  109.3 5.1 %collective-permute-start.3 = (bf16[10,1,256]{2,1,0:T(2,128)(2,1)S(1)}, bf16[10,1,256]{2,1,0:T(2,128)(2,1)S(1)}, u32[]{:S(2)}, u32[]{:S(2)}) collective-permute-start(bf16[10,1,256]{2,1,0:T(2,128)(2,1)S(1)} %get-tuple-element.20), channel_id=1, source_target_pairs={{0,1},{1,2},{2,3},{3,4},{4,5},{5,6},{6,7},{8,9},{9,10},{10,11},{11... | collective-permute-start | bytes 15368 | tf_op jit(solution)/shard_map/ppermute | solution.py:18
  115.4 52.3 %copy-start.10 = (bf16[12,16,256]{2,1,0:T(8,128)(2,1)S(1)}, bf16[12,16,256]{2,1,0:T(8,128)(2,1)}, u32[]{:S(2)}) copy-start(bf16[12,16,256]{2,1,0:T(8,128)(2,1)} %param.10) | copy-start | bytes 294916
  116.0 59.0 %copy-start.12 = (bf16[14,16,256]{2,1,0:T(8,128)(2,1)S(1)}, bf16[14,16,256]{2,1,0:T(8,128)(2,1)}, u32[]{:S(2)}) copy-start(bf16[14,16,256]{2,1,0:T(8,128)(2,1)} %copy-done.11) | copy-start | bytes 344068
  168.0 16.0 %collective-permute-start.4 = (bf16[1,16,256]{2,1,0:T(8,128)(2,1)S(1)}, bf16[1,16,256]{2,1,0:T(8,128)(2,1)S(1)}, u32[]{:S(2)}, u32[]{:S(2)}) collective-permute-start(bf16[1,16,256]{2,1,0:T(8,128)(2,1)S(1)} %get-tuple-element.33), channel_id=1, source_target_pairs={{0,8},{8,16},{16,24},{24,32},{32,40},{40,48},{48,56},{56,64},{64,7... | collective-permute-start | bytes 24584 | tf_op jit(solution)/shard_map/ppermute | solution.py:18
  172.9 11.0 %collective-permute-start.5 = (bf16[1,16,256]{2,1,0:T(8,128)(2,1)S(1)}, bf16[1,16,256]{2,1,0:T(8,128)(2,1)S(1)}, u32[]{:S(2)}, u32[]{:S(2)}) collective-permute-start(bf16[1,16,256]{2,1,0:T(8,128)(2,1)S(1)} %get-tuple-element.34), channel_id=1, source_target_pairs={{8,0},{16,8},{24,16},{32,24},{40,32},{48,40},{56,48},{64,56},{72,6... | collective-permute-start | bytes 24584 | tf_op jit(solution)/shard_map/ppermute | solution.py:20
  181.0 1.1 copy-start.6
  184.0 5.5 %collective-permute-start.6 = (bf16[14,1,256]{2,1,0:T(2,128)(2,1)S(1)}, bf16[14,1,256]{2,1,0:T(2,128)(2,1)S(1)}, u32[]{:S(2)}, u32[]{:S(2)}) collective-permute-start(bf16[14,1,256]{2,1,0:T(2,128)(2,1)S(1)} %get-tuple-element.25), channel_id=1, source_target_pairs={{1,0},{2,1},{3,2},{4,3},{5,4},{6,5},{7,6},{9,8},{10,9},{11,10},{12... | collective-permute-start | bytes 21512 | tf_op jit(solution)/shard_map/ppermute | solution.py:20
  185.3 4.8 %collective-permute-start.7 = (bf16[14,1,256]{2,1,0:T(2,128)(2,1)S(1)}, bf16[14,1,256]{2,1,0:T(2,128)(2,1)S(1)}, u32[]{:S(2)}, u32[]{:S(2)}) collective-permute-start(bf16[14,1,256]{2,1,0:T(2,128)(2,1)S(1)} %get-tuple-element.26), channel_id=1, source_target_pairs={{0,1},{1,2},{2,3},{3,4},{4,5},{5,6},{6,7},{8,9},{9,10},{10,11},{11... | collective-permute-start | bytes 21512 | tf_op jit(solution)/shard_map/ppermute | solution.py:18
  337.4 3.3 copy-start.1
Sparse Core Ops, SparseCore 0:
  40.5 39.0 reduce-scatter.2
  86.0 80.6 reduce-scatter.4
  184.0 153.2 all-reduce.1
where the time goes:
time: 349 us; the launch traced here: 347 us
  waiting for transfers between devices  196 us (56%)
  starting transfers between devices  47.5 us (14%)
  local copies, waits for them, and re-layouts  38.9 us (11%)
  matrix products  32.2 us (9%)
  other arithmetic  18.1 us (5%)
  between operations  14.6 us (4%)
    psum x1, waiting for transfers between devices, body(): weight_grad = lax.psum(local_weight, ('pb', 'ka'))  145 us
    reduce_scatter x1, waiting for transfers between devices, body(): lax.psum_scatter((fine_term + coarse_sum) * norm_scale, 'pb', scatter_dim...  49.9 us
    ppermute x8, starting transfers between devices, padded(): lax.ppermute(tail, axis, [(i, (i + 1) % count) for i in range(ends)])  34.2 us
    ppermute x8, starting transfers between devices, padded(): lax.ppermute(head, axis, [((i + 1) % count, i) for i in range(ends)])  13.2 us
    dot_general x4, matrix products, body(): jnp.dot(grad_block, ordered, preferred_element_type=jnp.float32)  12 us
    div x2, local copies, waits for them, and re-layouts, body(): coarse_sum = coarse_sum + spread / 4.0 ** level_index  10.2 us
    reduce_sum x3, other arithmetic, pool_levels(): pooled = strip_float.reshape(cell_cols // factor, factor, key_rows // fac...  9.77 us
    unnamed x32, local copies, waits for them, and re-layouts  8.44 us
  transfers between devices with their start and end apart: 19, of which 4 were waited for; matrix products, arithmetic and copies ran while one was open for 14% of the time, Pallas kernels for 0%

commit v1 on v0

--- a/solution.py
+++ b/solution.py
@@ -119,7 +119,9 @@
     grad_first, weight_first = conv_backward(padded_query_image, padded_query_grad, conv_weight)
     grad_second, weight_swapped = conv_backward(padded_key_image, padded_key_grad, kernel_swapped)
     local_weight = weight_first + jnp.transpose(weight_swapped, (1, 0, 2, 3))
-    weight_grad = lax.psum(local_weight, ("pb", "ka"))
+    weight_grad = local_weight
+    for src_i in ("ka", "pb"):
+        weight_grad = lax.psum(weight_grad, src_i)
     return (grad_first.astype(jnp.bfloat16), grad_second.astype(jnp.bfloat16), weight_grad)
 
 

time: 349 us -> 414 us (1.19)
  waiting for transfers between devices: 196 us -> 258 us
    psum x1 -> x2, waiting for transfers between devices: 145 us -> 210 us  [body(): weight_grad = lax.psum(weight_grad, src_i)]
    reduce_scatter x1, waiting for transfers between devices: 49.9 us -> 44.7 us  [body(): lax.psum_scatter((fine_term + coarse_sum) * norm_scale, 'pb', scatter_dim...]
    unnamed x32 -> x54, local copies, waits for them, and re-layouts: 8.44 us -> 10.1 us
  transfers between devices with their start and end apart: 19 -> 20, of which waited for: 4 -> 4; matrix products, arithmetic and copies ran while one was open for 14% -> 11% of each run, Pallas kernels for 0% -> 0%
where the time goes in v1:
time: 414 us; the launch traced here: 413 us
  waiting for transfers between devices  258 us (62%)
  starting transfers between devices  47.5 us (11%)
  local copies, waits for them, and re-layouts  41.8 us (10%)
  matrix products  32.4 us (8%)
  other arithmetic  18.7 us (5%)
  between operations  14.8 us (4%)
    psum x2, waiting for transfers between devices, body(): weight_grad = lax.psum(weight_grad, src_i)  210 us
    reduce_scatter x1, waiting for transfers between devices, body(): lax.psum_scatter((fine_term + coarse_sum) * norm_scale, 'pb', scatter_dim...  44.7 us
    ppermute x8, starting transfers between devices, padded(): lax.ppermute(tail, axis, [(i, (i + 1) % count) for i in range(ends)])  34.2 us
    ppermute x8, starting transfers between devices, padded(): lax.ppermute(head, axis, [((i + 1) % count, i) for i in range(ends)])  13.2 us
    dot_general x4, matrix products, body(): jnp.dot(grad_block, ordered, preferred_element_type=jnp.float32)  12 us
    div x2, local copies, waits for them, and re-layouts, body(): coarse_sum = coarse_sum + spread / 4.0 ** level_index  10.2 us
    unnamed x54, local copies, waits for them, and re-layouts  10.1 us
    reduce_sum x3, other arithmetic, pool_levels(): pooled = strip_float.reshape(cell_cols // factor, factor, key_rows // fac...  9.77 us
  transfers between devices with their start and end apart: 20, of which 4 were waited for; matrix products, arithmetic and copies ran while one was open for 11% of the time, Pallas kernels for 0%

profile of v1, /device:TPU:1, one launch (start us, length us, event | category | flops | bytes accessed | tf_op | source)
XLA Modules:
  0.0 412.9 jit_solution(15425581410795200754)
XLA Ops:
  7.2 4.6 %reshape.140 = f32[96,2,8,2,256]{4,3,2,1,0:T(2,128)} reshape(bf16[192,16,256]{2,1,0:T(8,128)(2,1)} %param.7) | data formatting | bytes 4718592 | tf_op jit(solution)/shard_map/reshape | solution.py:33
  11.8 1.7 copy.47
  13.5 2.5 reshape.142
  15.9 2.2 convert_element_type.43
  18.1 4.4 %reduce_sum.27 = f32[96,8,256]{2,1,0:T(8,128)S(1)} reduce(f32[96,2,8,2,256]{4,3,2,1,0:T(2,128)} %reshape.140, f32[]{:T(128)} %constant.6.clone.1), dimensions={1,3}, to_apply=%region_0.0 | reduce | flops 589824 | bytes 3932164 | tf_op jit(solution)/shard_map/reduce_sum | solution.py:35
  22.7 3.0 reduce_sum.32
  25.7 2.4 reduce_sum.33
  28.2 2.8 convolution_bitcast_fusion.2
  31.0 5.2 %fusion.4 = f32[1536,256]{1,0:T(8,128)S(1)} fusion(f32[1536,256]{1,0:T(8,128)S(1)} %convolution_bitcast_fusion.2, bf16[3072,256]{1,0:T(8,128)(2,1)S(1)} %bitcast.277, bf16[1536,4080]{0,1:T(8,128)(2,1)} %bitcast.279), kind=kOutput, calls=%fused_computation.5 | convolution fusion | flops 2416312320 | bytes 14155776 | tf_op jit(solution)/shard_map/dot_general | solution.py:90
  36.2 1.5 fusion.9
  37.8 2.5 fusion.8
  41.1 4.6 %collective-permute-start.12 = (bf16[1,16,256]{2,1,0:T(8,128)(2,1)S(1)}, bf16[1,16,256]{2,1,0:T(8,128)(2,1)S(1)}, u32[]{:S(2)}, u32[]{:S(2)}) collective-permute-start(bf16[1,16,256]{2,1,0:T(8,128)(2,1)S(1)} %get-tuple-element.28), channel_id=1, source_target_pairs={{0,8},{8,16},{16,24},{24,32},{32,40},{40,48},{48,56},{56,64},{64,7... | collective-permute-start | bytes 24584 | tf_op jit(solution)/shard_map/ppermute | solution.py:18
  45.7 2.1 collective-permute-start.13
  47.8 1.8 slice.313
  49.7 1.1 slice.314
  52.5 2.9 broadcast_in_dim.6
  55.4 5.2 %div.61 = f32[192,16,256]{2,0,1:T(8,128)} reshape(f32[96,2,8,2,256]{4,1,0,3,2:T(2,128)} %broadcast_in_dim.6) | data formatting | bytes 6291456 | tf_op jit(solution)/shard_map/div | solution.py:101
  61.0 2.3 broadcast_in_dim.7
  63.3 4.9 %div.65 = f32[192,16,256]{2,0,1:T(8,128)} reshape(f32[48,4,4,4,256]{4,1,0,3,2:T(4,128)} %broadcast_in_dim.7) | data formatting | bytes 6291456 | tf_op jit(solution)/shard_map/div | solution.py:101
  68.4 5.4 %fusion = f32[256,3072]{0,1:S(1)} fusion(bf16[1536,256]{1,0:T(8,128)(2,1)S(1)} %bitcast.256, bf16[1536,4080]{0,1:T(8,128)(2,1)} %bitcast.285), kind=kOutput, calls=%fused_computation | convolution fusion | flops 2415919104 | bytes 13369344
  74.2 1.6 copy-done.3
  75.8 1.0 add_multiply_fusion
  76.7 3.5 copy.54
  81.1 3.6 collective-permute-start.8
  84.7 1.9 collective-permute-start.9
  87.3 3.7 collective-permute-start.14
  91.1 1.3 collective-permute-start.15
  92.4 1.3 collective-permute-start.11
  93.7 4.6 %collective-permute-start.10 = (bf16[10,1,256]{2,1,0:T(2,128)(2,1)S(1)}, bf16[10,1,256]{2,1,0:T(2,128)(2,1)S(1)}, u32[]{:S(2)}, u32[]{:S(2)}) collective-permute-start(bf16[10,1,256]{2,1,0:T(2,128)(2,1)S(1)} %get-tuple-element.15), channel_id=1, source_target_pairs={{0,1},{1,2},{2,3},{3,4},{4,5},{5,6},{6,7},{8,9},{9,10},{10,11},{11... | collective-permute-start | bytes 15368 | tf_op jit(solution)/shard_map/ppermute | solution.py:18
  98.4 0.9 convert_element_type.50
  99.4 4.5 %collective-permute-start = (bf16[1,24,256]{2,1,0:T(8,128)(2,1)S(1)}, bf16[1,24,256]{2,1,0:T(8,128)(2,1)S(1)}, u32[]{:S(2)}, u32[]{:S(2)}) collective-permute-start(bf16[1,24,256]{2,1,0:T(8,128)(2,1)S(1)} %get-tuple-element.37), channel_id=1, source_target_pairs={{0,8},{8,16},{16,24},{24,32},{32,40},{40,48},{48,56},{56,64},{64,7... | collective-permute-start | bytes 36872 | tf_op jit(solution)/shard_map/ppermute | solution.py:18
  103.9 1.9 collective-permute-start.1
  107.3 1.1 maximum_bitcast_fusion.1
  109.2 1.4 collective-permute-start.2
  110.6 4.3 %collective-permute-start.3 = (bf16[10,1,256]{2,1,0:T(2,128)(2,1)S(1)}, bf16[10,1,256]{2,1,0:T(2,128)(2,1)S(1)}, u32[]{:S(2)}, u32[]{:S(2)}) collective-permute-start(bf16[10,1,256]{2,1,0:T(2,128)(2,1)S(1)} %get-tuple-element.20), channel_id=1, source_target_pairs={{0,1},{1,2},{2,3},{3,4},{4,5},{5,6},{6,7},{8,9},{9,10},{10,11},{11... | collective-permute-start | bytes 15368 | tf_op jit(solution)/shard_map/ppermute | solution.py:18
  116.7 44.7 %reduce-scatter.5.cloned.1.call-done = f32[12,16,256]{2,1,0:T(8,128)} async-done(((f32[192,16,256]{2,1,0:T(8,128)}), f32[12,16,256]{2,1,0:T(8,128)}) %reduce-scatter.5.cloned.1.call-update) | async-done | bytes 196624 | tf_op jit(solution)/shard_map/reduce_scatter | solution.py:109
  162.8 1.1 convolution_bitcast_fusion.7
  167.8 0.9 convolution_bitcast_fusion.9
  169.1 1.0 copy-done.6
  170.1 1.7 maximum_add_fusion
  174.3 4.9 %collective-permute-start.4 = (bf16[1,16,256]{2,1,0:T(8,128)(2,1)S(1)}, bf16[1,16,256]{2,1,0:T(8,128)(2,1)S(1)}, u32[]{:S(2)}, u32[]{:S(2)}) collective-permute-start(bf16[1,16,256]{2,1,0:T(8,128)(2,1)S(1)} %get-tuple-element.33), channel_id=1, source_target_pairs={{0,8},{8,16},{16,24},{24,32},{32,40},{40,48},{48,56},{56,64},{64,7... | collective-permute-start | bytes 24584 | tf_op jit(solution)/shard_map/ppermute | solution.py:18
  179.3 1.9 collective-permute-start.5
  182.1 2.6 collective-permute-done.5
  184.7 1.3 collective-permute-start.6
  186.0 4.0 collective-permute-start.7
  190.0 62.1 %all-reduce.3.cloned.1.call-done = f32[3,3,256,256]{3,2,1,0:T(8,128)} async-done(((f32[3,3,256,256]{3,2,1,0:T(8,128)}), f32[3,3,256,256]{3,2,1,0:T(8,128)}) %all-reduce.3.cloned.1.call-update) | async-done | bytes 2359312 | tf_op jit(solution)/shard_map/psum | solution.py:124
  254.8 148.2 %all-reduce.5.cloned.1.call-done = f32[3,3,256,256]{3,2,1,0:T(8,128)} async-done(((f32[3,3,256,256]{3,2,1,0:T(8,128)}), f32[3,3,256,256]{3,2,1,0:T(8,128)}) %all-reduce.5.cloned.1.call-update) | async-done | bytes 2359312 | tf_op jit(solution)/shard_map/psum | solution.py:124
  403.1 3.3 copy.74
  (139 shorter events, 20.8 us)
Async XLA Ops:
  7.2 44.5 %copy-start = (bf16[8,192,256]{2,1,0:T(8,128)(2,1)S(1)}, bf16[8,192,256]{2,1,0:T(8,128)(2,1)}, u32[]{:S(2)}) copy-start(bf16[8,192,256]{2,1,0:T(8,128)(2,1)} %param.6) | copy-start | bytes 2359300
  7.2 4.6 %copy-start.2 = (bf16[192,16,256]{2,1,0:T(8,128)(2,1)S(1)}, bf16[192,16,256]{2,1,0:T(8,128)(2,1)}, u32[]{:S(2)}) copy-start(bf16[192,16,256]{2,1,0:T(8,128)(2,1)} %param.7) | copy-start | bytes 4718596
  7.2 91.2 %reduce-scatter.3.cloned.1.call-start = ((), (), s32[]{:S(2)}) async-start(), calls=%async_computation.2 | async-start | bytes 1769472 | tf_op jit(solution)/shard_map/reduce_scatter | solution.py:102
  28.2 2.8 copy-start.7
  40.2 0.9 copy-start.9
  40.3 121.1 %reduce-scatter.5.cloned.1.call-start = ((), (), s32[]{:S(2)}) async-start(), calls=%async_computation.3 | async-start | bytes 3342336 | tf_op jit(solution)/shard_map/reduce_scatter | solution.py:109
  41.1 45.5 %collective-permute-start.12 = (bf16[1,16,256]{2,1,0:T(8,128)(2,1)S(1)}, bf16[1,16,256]{2,1,0:T(8,128)(2,1)S(1)}, u32[]{:S(2)}, u32[]{:S(2)}) collective-permute-start(bf16[1,16,256]{2,1,0:T(8,128)(2,1)S(1)} %get-tuple-element.28), channel_id=1, source_target_pairs={{0,8},{8,16},{16,24},{24,32},{32,40},{40,48},{48,56},{56,64},{64,7... | collective-permute-start | bytes 24584 | tf_op jit(solution)/shard_map/ppermute | solution.py:18
  45.7 41.0 %collective-permute-start.13 = (bf16[1,16,256]{2,1,0:T(8,128)(2,1)S(1)}, bf16[1,16,256]{2,1,0:T(8,128)(2,1)S(1)}, u32[]{:S(2)}, u32[]{:S(2)}) collective-permute-start(bf16[1,16,256]{2,1,0:T(8,128)(2,1)S(1)} %get-tuple-element.27), channel_id=1, source_target_pairs={{8,0},{16,8},{24,16},{32,24},{40,32},{48,40},{56,48},{64,56},{72,6... | collective-permute-start | bytes 24584 | tf_op jit(solution)/shard_map/ppermute | solution.py:20
  68.4 5.7 %copy-start.4 = (f32[192,16,256]{2,0,1:T(8,128)S(1)}, f32[192,16,256]{2,0,1:T(8,128)}, u32[]{:S(2)}) copy-start(f32[192,16,256]{2,0,1:T(8,128)} %div.65) | copy-start | bytes 9437188
  73.8 1.9 copy-start.3
  80.2 0.9 copy-start.8
  80.2 171.8 %all-reduce.3.cloned.1.call-start = ((), (), s32[]{:S(2)}) async-start(), calls=%async_computation.4 | async-start | bytes 4718592 | tf_op jit(solution)/shard_map/psum | solution.py:124
  81.1 11.3 %collective-permute-start.8 = (bf16[1,24,256]{2,1,0:T(8,128)(2,1)S(1)}, bf16[1,24,256]{2,1,0:T(8,128)(2,1)S(1)}, u32[]{:S(2)}, u32[]{:S(2)}) collective-permute-start(bf16[1,24,256]{2,1,0:T(8,128)(2,1)S(1)} %get-tuple-element.30), channel_id=1, source_target_pairs={{0,8},{8,16},{16,24},{24,32},{32,40},{40,48},{48,56},{56,64},{64,7... | collective-permute-start | bytes 36872 | tf_op jit(solution)/shard_map/ppermute | solution.py:18
  84.7 7.7 %collective-permute-start.9 = (bf16[1,24,256]{2,1,0:T(8,128)(2,1)S(1)}, bf16[1,24,256]{2,1,0:T(8,128)(2,1)S(1)}, u32[]{:S(2)}, u32[]{:S(2)}) collective-permute-start(bf16[1,24,256]{2,1,0:T(8,128)(2,1)S(1)} %get-tuple-element.29), channel_id=1, source_target_pairs={{8,0},{16,8},{24,16},{32,24},{40,32},{48,40},{56,48},{64,56},{72,6... | collective-permute-start | bytes 36872 | tf_op jit(solution)/shard_map/ppermute | solution.py:20
  86.6 19.9 %copy-start.20 = (bf16[1,16,256]{2,1,0:T(8,128)(2,1)}, bf16[1,16,256]{2,1,0:T(8,128)(2,1)S(1)}, u32[]{:S(2)}) copy-start(bf16[1,16,256]{2,1,0:T(8,128)(2,1)S(1)} %collective-permute-done.12) | copy-start | bytes 24580
  86.7 19.9 %copy-start.22 = (bf16[1,16,256]{2,1,0:T(8,128)(2,1)}, bf16[1,16,256]{2,1,0:T(8,128)(2,1)S(1)}, u32[]{:S(2)}) copy-start(bf16[1,16,256]{2,1,0:T(8,128)(2,1)S(1)} %collective-permute-done.13) | copy-start | bytes 24580
  86.7 17.2 %copy-start.18 = (bf16[14,16,256]{2,1,0:T(8,128)(2,1)}, bf16[14,16,256]{2,1,0:T(8,128)(2,1)S(1)}, u32[]{:S(2)}) copy-start(bf16[14,16,256]{2,1,0:T(8,128)(2,1)S(1)} %constant_dynamic-update-slice_fusion.3) | copy-start | bytes 344068
  87.3 76.6 %collective-permute-start.14 = (bf16[14,1,256]{2,1,0:T(2,128)(2,1)S(1)}, bf16[14,1,256]{2,1,0:T(2,128)(2,1)}, u32[]{:S(2)}, u32[]{:S(2)}) collective-permute-start(bf16[14,1,256]{2,1,0:T(2,128)(2,1)S(1)} %get-tuple-element.21), channel_id=1, source_target_pairs={{0,1},{1,2},{2,3},{3,4},{4,5},{5,6},{6,7},{8,9},{9,10},{10,11},{11... | collective-permute-start | bytes 21512 | tf_op jit(solution)/shard_map/ppermute | solution.py:18
  91.1 71.7 %collective-permute-start.15 = (bf16[14,1,256]{2,1,0:T(2,128)(2,1)}, bf16[14,1,256]{2,1,0:T(2,128)(2,1)}, u32[]{:S(2)}, u32[]{:S(2)}) collective-permute-start(bf16[14,1,256]{2,1,0:T(2,128)(2,1)} %get-tuple-element.22), channel_id=1, source_target_pairs={{1,0},{2,1},{3,2},{4,3},{5,4},{6,5},{7,6},{9,8},{10,9},{11,10},{12... | collective-permute-start | bytes 21512 | tf_op jit(solution)/shard_map/ppermute | solution.py:20
  92.4 11.4 %collective-permute-start.11 = (bf16[10,1,256]{2,1,0:T(2,128)(2,1)S(1)}, bf16[10,1,256]{2,1,0:T(2,128)(2,1)S(1)}, u32[]{:S(2)}, u32[]{:S(2)}) collective-permute-start(bf16[10,1,256]{2,1,0:T(2,128)(2,1)S(1)} %get-tuple-element.16), channel_id=1, source_target_pairs={{1,0},{2,1},{3,2},{4,3},{5,4},{6,5},{7,6},{9,8},{10,9},{11,10},{12... | collective-permute-start | bytes 15368 | tf_op jit(solution)/shard_map/ppermute | solution.py:20
  93.7 12.5 %collective-permute-start.10 = (bf16[10,1,256]{2,1,0:T(2,128)(2,1)S(1)}, bf16[10,1,256]{2,1,0:T(2,128)(2,1)S(1)}, u32[]{:S(2)}, u32[]{:S(2)}) collective-permute-start(bf16[10,1,256]{2,1,0:T(2,128)(2,1)S(1)} %get-tuple-element.15), channel_id=1, source_target_pairs={{0,1},{1,2},{2,3},{3,4},{4,5},{5,6},{6,7},{8,9},{9,10},{10,11},{11... | collective-permute-start | bytes 15368 | tf_op jit(solution)/shard_map/ppermute | solution.py:18
  99.4 9.8 %collective-permute-start = (bf16[1,24,256]{2,1,0:T(8,128)(2,1)S(1)}, bf16[1,24,256]{2,1,0:T(8,128)(2,1)S(1)}, u32[]{:S(2)}, u32[]{:S(2)}) collective-permute-start(bf16[1,24,256]{2,1,0:T(8,128)(2,1)S(1)} %get-tuple-element.37), channel_id=1, source_target_pairs={{0,8},{8,16},{16,24},{24,32},{32,40},{40,48},{48,56},{56,64},{64,7... | collective-permute-start | bytes 36872 | tf_op jit(solution)/shard_map/ppermute | solution.py:18
  103.9 5.3 %collective-permute-start.1 = (bf16[1,24,256]{2,1,0:T(8,128)(2,1)S(1)}, bf16[1,24,256]{2,1,0:T(8,128)(2,1)S(1)}, u32[]{:S(2)}, u32[]{:S(2)}) collective-permute-start(bf16[1,24,256]{2,1,0:T(8,128)(2,1)S(1)} %get-tuple-element.38), channel_id=1, source_target_pairs={{8,0},{16,8},{24,16},{32,24},{40,32},{48,40},{56,48},{64,56},{72,6... | collective-permute-start | bytes 36872 | tf_op jit(solution)/shard_map/ppermute | solution.py:20
  108.8 6.7 %copy-start.5 = (bf16[3,3,256,256]{3,2,1,0:T(8,128)(2,1)S(1)}, bf16[3,3,256,256]{3,2,1,0:T(8,128)(2,1)}, u32[]{:S(2)}) copy-start(bf16[3,3,256,256]{3,2,1,0:T(8,128)(2,1)} %param.11) | copy-start | bytes 3538948
  109.1 53.2 %copy-start.10 = (bf16[12,16,256]{2,1,0:T(8,128)(2,1)S(1)}, bf16[12,16,256]{2,1,0:T(8,128)(2,1)}, u32[]{:S(2)}) copy-start(bf16[12,16,256]{2,1,0:T(8,128)(2,1)} %param.10) | copy-start | bytes 294916
  109.2 6.6 %collective-permute-start.2 = (bf16[10,1,256]{2,1,0:T(2,128)(2,1)S(1)}, bf16[10,1,256]{2,1,0:T(2,128)(2,1)S(1)}, u32[]{:S(2)}, u32[]{:S(2)}) collective-permute-start(bf16[10,1,256]{2,1,0:T(2,128)(2,1)S(1)} %get-tuple-element.19), channel_id=1, source_target_pairs={{1,0},{2,1},{3,2},{4,3},{5,4},{6,5},{7,6},{9,8},{10,9},{11,10},{12... | collective-permute-start | bytes 15368 | tf_op jit(solution)/shard_map/ppermute | solution.py:20
  110.6 51.9 %copy-start.23 = (bf16[1,16,256]{2,1,0:T(8,128)(2,1)S(1)}, bf16[1,16,256]{2,1,0:T(8,128)(2,1)}, u32[]{:S(2)}) copy-start(bf16[1,16,256]{2,1,0:T(8,128)(2,1)} %copy-done.22) | copy-start | bytes 24580
  110.6 5.1 %collective-permute-start.3 = (bf16[10,1,256]{2,1,0:T(2,128)(2,1)S(1)}, bf16[10,1,256]{2,1,0:T(2,128)(2,1)S(1)}, u32[]{:S(2)}, u32[]{:S(2)}) collective-permute-start(bf16[10,1,256]{2,1,0:T(2,128)(2,1)S(1)} %get-tuple-element.20), channel_id=1, source_target_pairs={{0,1},{1,2},{2,3},{3,4},{4,5},{5,6},{6,7},{8,9},{9,10},{10,11},{11... | collective-permute-start | bytes 15368 | tf_op jit(solution)/shard_map/ppermute | solution.py:18
  162.3 1.7 copy-start.19
  166.9 1.9 copy-start.21
  169.0 1.1 copy-start.6
  171.9 0.9 copy-start.16
  171.9 1.1 copy-start.15
  171.9 1.3 copy-start.14
  171.9 1.6 copy-start.13
  171.9 2.0 copy-start.12
  171.9 231.2 %all-reduce.5.cloned.1.call-start = ((), (), s32[]{:S(2)}) async-start(), calls=%async_computation.5 | async-start | bytes 4718592 | tf_op jit(solution)/shard_map/psum | solution.py:124
  172.9 1.1 copy-start.11
  173.2 8.0 %copy-start.17 = (bf16[8,24,256]{2,1,0:T(8,128)(2,1)S(1)}, bf16[8,24,256]{2,1,0:T(8,128)(2,1)}, u32[]{:S(2)}) copy-start(bf16[8,24,256]{2,1,0:T(8,128)(2,1)} %get-tuple-element.35) | copy-start | bytes 294916
  174.3 7.7 %collective-permute-start.4 = (bf16[1,16,256]{2,1,0:T(8,128)(2,1)S(1)}, bf16[1,16,256]{2,1,0:T(8,128)(2,1)S(1)}, u32[]{:S(2)}, u32[]{:S(2)}) collective-permute-start(bf16[1,16,256]{2,1,0:T(8,128)(2,1)S(1)} %get-tuple-element.33), channel_id=1, source_target_pairs={{0,8},{8,16},{16,24},{24,32},{32,40},{40,48},{48,56},{56,64},{64,7... | collective-permute-start | bytes 24584 | tf_op jit(solution)/shard_map/ppermute | solution.py:18
  179.3 5.4 %collective-permute-start.5 = (bf16[1,16,256]{2,1,0:T(8,128)(2,1)S(1)}, bf16[1,16,256]{2,1,0:T(8,128)(2,1)S(1)}, u32[]{:S(2)}, u32[]{:S(2)}) collective-permute-start(bf16[1,16,256]{2,1,0:T(8,128)(2,1)S(1)} %get-tuple-element.34), channel_id=1, source_target_pairs={{8,0},{16,8},{24,16},{32,24},{40,32},{48,40},{56,48},{64,56},{72,6... | collective-permute-start | bytes 24584 | tf_op jit(solution)/shard_map/ppermute | solution.py:20
  184.7 67.6 %collective-permute-start.6 = (bf16[14,1,256]{2,1,0:T(2,128)(2,1)S(1)}, bf16[14,1,256]{2,1,0:T(2,128)(2,1)S(1)}, u32[]{:S(2)}, u32[]{:S(2)}) collective-permute-start(bf16[14,1,256]{2,1,0:T(2,128)(2,1)S(1)} %get-tuple-element.25), channel_id=1, source_target_pairs={{1,0},{2,1},{3,2},{4,3},{5,4},{6,5},{7,6},{9,8},{10,9},{11,10},{12... | collective-permute-start | bytes 21512 | tf_op jit(solution)/shard_map/ppermute | solution.py:20
  186.0 66.3 %collective-permute-start.7 = (bf16[14,1,256]{2,1,0:T(2,128)(2,1)S(1)}, bf16[14,1,256]{2,1,0:T(2,128)(2,1)S(1)}, u32[]{:S(2)}, u32[]{:S(2)}) collective-permute-start(bf16[14,1,256]{2,1,0:T(2,128)(2,1)S(1)} %get-tuple-element.26), channel_id=1, source_target_pairs={{0,1},{1,2},{2,3},{3,4},{4,5},{5,6},{6,7},{8,9},{9,10},{10,11},{11... | collective-permute-start | bytes 21512 | tf_op jit(solution)/shard_map/ppermute | solution.py:18
  403.1 3.3 copy-start.1
Sparse Core Ops, SparseCore 0:
  40.4 38.8 reduce-scatter.2
  83.3 77.9 reduce-scatter.4
  172.0 79.9 all-reduce.2
  254.4 148.6 all-reduce.4
